TPU v7x, 32 devices: a whole 2x2x4 slice. The times are simulated.
32 devices in a mesh: node: 8 (over z, y), rep: 4 (over x, core).
Axes of the slice: x: 2, y: 2, z: 4, core: 2. Of those that a mesh axis runs over, the one named last changes fastest.
Arguments:
- features: bfloat16 [16384, 256], P('node'), may hold values from -6 to 6
- tiles: bfloat16 [8, 4, 4, 96, 128, 128], P('node', 'rep'), may hold values from -0.09375 to 0.09375
- tile_rows: int32 [8, 4, 4, 96], P('node', 'rep'), may hold values from 0 to 15
- tile_cols: int32 [8, 4, 4, 96], P('node', 'rep'), may hold values from 0 to 15
- tile_count: int32 [8, 4, 4], P('node', 'rep'), may hold values from 1 to 96, as said below
- order: int32 [16384], P('node'), may hold values from 0 to 16383, as said below
- weight: bfloat16 [256, 256], replicated, may hold values from -0.375 to 0.375
- cotangent: bfloat16 [16384, 256], P(('node', 'rep')), may hold values from -6 to 6
Outputs:
- activated: bfloat16 [16384, 256], P(('node', 'rep'))
- feature_grad: bfloat16 [16384, 256], P(('node', 'rep'))
- weight_grad: float32 [256, 256], replicated
Inputs may be any that keep to these rules, and one draw needn't show every extreme that they name: `tile_count`: for every node block and offset, exactly one tile group holds 96 live slots; the counts of the others lie between 1 and 32. order is a permutation of the nodes that maps each aligned block of 512 positions onto itself.
All inputs are finite; a program needn't handle non-finite values.
Results may differ from a plain program's by a relative error of at most 0.017.
Values may be sent and summed in bfloat16 or wider, within the bound.
A program may use at most 128 MiB of HBM per device.

v0:
```python
import functools
import math

import jax
import jax.numpy as jnp
from jax import lax
from jax.experimental import pallas as pl
from jax.experimental.pallas import tpu as pltpu
from jax.sharding import PartitionSpec as P

CHUNK = 8
GROUP = 4


def from_behind(block, axis, distance):
    n = lax.axis_size(axis)
    return lax.ppermute(block, axis, [((i - distance) % n, i) for i in range(n)])


def stream(tiles, held, sems, count_ref, ks, step):
    chunks = tiles.shape[1] // CHUNK

    def copy(j, c):
        return pltpu.make_async_copy(
            tiles.at[ks[j], pl.ds(c * CHUNK, CHUNK)],
            held.at[j, pl.ds(c * CHUNK, CHUNK)],
            sems.at[j * chunks + c],
        )

    for j, k in enumerate(ks):
        live = lax.div(count_ref[k] + (CHUNK - 1), CHUNK)

        def begin(c, _, j=j):
            copy(j, c).start()
            return 0

        lax.fori_loop(0, live, begin, 0)
    for j, k in enumerate(ks):
        before, body, after = step(j, k)
        before()
        full = lax.div(count_ref[k], CHUNK)
        rest = count_ref[k] - full * CHUNK

        def whole(c, _, j=j):
            copy(j, c).wait()
            for g in range(0, CHUNK, GROUP):
                body([c * CHUNK + g + i for i in range(GROUP)])
            return 0

        lax.fori_loop(0, full, whole, 0)

        @pl.when(rest > 0)
        def _(j=j):
            copy(j, full).wait()

            def one(s, _):
                body([full * CHUNK + s])
                return 0

            lax.fori_loop(0, rest, one, 0)

        after()


def forward_kernel(ks, capacity, seeded, *refs):
    if seeded:
        count_ref, row_ref, col_ref, tiles, source, seed, out, held, acc, sems = refs
    else:
        count_ref, row_ref, col_ref, tiles, source, out, held, acc, sems = refs
    per = source.shape[2]
    if seeded:
        acc[...] = seed[...]
    else:
        acc[...] = jnp.zeros_like(acc)

    def step(j, k):
        def body(slots):
            products, puts = [], []
            for s in slots:
                col = col_ref[k * capacity + s]
                puts.append(row_ref[k * capacity + s])
                products.append(
                    jnp.dot(
                        held[j, s],
                        source[lax.div(col, per), j, lax.rem(col, per)],
                        preferred_element_type=jnp.float32,
                    )
                )
            for put, product in zip(puts, products):
                acc[put] += product

        return (lambda: None), body, (lambda: None)

    stream(tiles, held, sems, count_ref, ks, step)
    out[...] = acc[...].astype(out.dtype)


def backward_kernel(ks, capacity, count_ref, row_ref, col_ref, tiles, source, out, held, acc, sems):
    per = out.shape[2]

    def step(j, k):
        def before():
            acc[...] = jnp.zeros_like(acc)

        def body(slots):
            products, puts = [], []
            for s in slots:
                puts.append(col_ref[k * capacity + s])
                products.append(
                    lax.dot_general(
                        held[j, s],
                        source[row_ref[k * capacity + s]],
                        (((0,), (0,)), ((), ())),
                        preferred_element_type=jnp.float32,
                    )
                )
            for put, product in zip(puts, products):
                acc[put] += product

        def after():
            for q in range(out.shape[0]):
                out[q, j] = acc[q * per : (q + 1) * per].astype(out.dtype)

        return before, body, after

    stream(tiles, held, sems, count_ref, ks, step)


def tile_call(kernel, ks, out_shape, out_dtype, acc_shape, args, tiles):
    capacity, size = tiles.shape[1], tiles.shape[-1]
    smem = pl.BlockSpec(memory_space=pltpu.SMEM)
    vmem = pl.BlockSpec(memory_space=pltpu.VMEM)
    return pl.pallas_call(
        kernel,
        out_shape=jax.ShapeDtypeStruct(out_shape, out_dtype),
        in_specs=[smem] * 3 + [pl.BlockSpec(memory_space=pl.ANY)] + [vmem] * (len(args) - 4),
        out_specs=vmem,
        scratch_shapes=[
            pltpu.VMEM((len(ks), capacity, size, size), tiles.dtype),
            pltpu.VMEM(acc_shape, jnp.float32),
            pltpu.SemaphoreType.DMA((len(ks) * (capacity // CHUNK),)),
        ],
        compiler_params=pltpu.CompilerParams(vmem_limit_bytes=60 * 1024 * 1024),
    )(*args)


def local(features, tiles, tile_rows, tile_cols, tile_count, order, weight, cotangent):
    rows_dev, feat = features.shape
    size = tiles.shape[-1]
    blocks = rows_dev // size
    quarter = cotangent.shape[0]
    reps = lax.axis_size("rep")
    per = blocks // reps
    rep_pos = lax.axis_index("rep")
    tile_set = tiles[0, 0]
    capacity = tile_set.shape[1]
    row_ids = tile_rows.reshape(-1)
    col_ids = tile_cols.reshape(-1)
    counts = tile_count.reshape(-1)

    within = (order % quarter).reshape(reps, quarter)
    spots = jnp.arange(quarter, dtype=jnp.int32)
    my_order = lax.dynamic_index_in_dim(within, rep_pos, 0, keepdims=False)
    my_pick = (my_order[:, None] == spots[None, :]).astype(jnp.bfloat16)
    my_features = lax.dynamic_slice_in_dim(features, rep_pos * quarter, quarter, 0)
    mine = jnp.dot(my_pick, my_features, preferred_element_type=jnp.float32).astype(jnp.bfloat16)
    halo = jnp.stack([from_behind(mine, "node", d) for d in (-1, 1, 2)])
    gathered = lax.all_gather(halo, "rep", axis=0)
    gathered = gathered.reshape(reps, 3, per, size, feat)

    pick = (within[:, :, None] == spots[None, None, :]).astype(jnp.bfloat16)
    here = jnp.einsum(
        "qpi,qif->qpf",
        pick,
        features.reshape(reps, quarter, feat),
        preferred_element_type=jnp.float32,
    ).astype(jnp.bfloat16)
    here = here.reshape(reps, 1, per, size, feat)

    acc_shape = (blocks, size, feat)
    scalars = (counts, row_ids, col_ids, tile_set)
    own = tile_call(
        functools.partial(forward_kernel, (1,), capacity, False),
        (1,), acc_shape, jnp.float32, acc_shape, scalars + (here,), tile_set,
    )
    partial_value = tile_call(
        functools.partial(forward_kernel, (0, 2, 3), capacity, True),
        (0, 2, 3), acc_shape, jnp.bfloat16, acc_shape, scalars + (gathered, own), tile_set,
    )
    aggregate = lax.psum_scatter(
        partial_value.reshape(rows_dev, feat), "rep", scatter_dimension=0, tiled=True
    )
    pre_act = jnp.dot(aggregate, weight, preferred_element_type=jnp.float32)
    gate_val = jax.nn.sigmoid(pre_act)
    activated = (pre_act * gate_val).astype(jnp.bfloat16)
    pre_grad = (
        cotangent.astype(jnp.float32) * gate_val * (1.0 + pre_act * (1.0 - gate_val))
    ).astype(jnp.bfloat16)
    back_rows = lax.dot_general(
        pre_grad, weight, (((1,), (1,)), ((), ())), preferred_element_type=jnp.float32
    ).astype(jnp.bfloat16)
    full_back = lax.all_gather(back_rows, "rep", axis=0, tiled=True).reshape(blocks, size, feat)
    weight_part = lax.dot_general(
        aggregate, pre_grad, (((0,), (0,)), ((), ())), preferred_element_type=jnp.float32
    )
    grad_scale = 1.0 / math.sqrt(rows_dev * lax.axis_size("node"))
    weight_grad = lax.psum(weight_part, ("node", "rep")) * grad_scale

    away = tile_call(
        functools.partial(backward_kernel, (0, 2, 3), capacity),
        (0, 2, 3), (reps, 3, per, size, feat), jnp.bfloat16, acc_shape, scalars + (full_back,), tile_set,
    )
    home = tile_call(
        functools.partial(backward_kernel, (1,), capacity),
        (1,), (reps, 1, per, size, feat), jnp.bfloat16, acc_shape, scalars + (full_back,), tile_set,
    )
    away = lax.psum_scatter(away.reshape(reps, 3 * quarter, feat), "rep", scatter_dimension=0)
    home = lax.psum_scatter(home.reshape(rows_dev, feat), "rep", scatter_dimension=0, tiled=True)
    away = away.reshape(3, quarter, feat)
    total = home.astype(jnp.float32)
    for j, d in enumerate((1, -1, -2)):
        total = total + from_behind(away[j], "node", d).astype(jnp.float32)
    feature_grad = lax.dot_general(
        my_pick, total.astype(jnp.bfloat16), (((0,), (0,)), ((), ())), preferred_element_type=jnp.float32
    ).astype(jnp.bfloat16)
    return (activated, feature_grad, weight_grad)


def solution(mesh):
    placed = (
        P("node", None),
        P("node", "rep", None, None, None, None),
        P("node", "rep", None, None),
        P("node", "rep", None, None),
        P("node", "rep", None),
        P("node"),
        P(),
        P(("node", "rep"), None),
    )
    return jax.shard_map(
        local,
        mesh=mesh,
        in_specs=placed,
        out_specs=(P(("node", "rep"), None), P(("node", "rep"), None), P()),
        check_vma=False,
    )
```

profile of v0, /device:TPU:1, one launch (start us, length us, event | category | flops | bytes accessed | tf_op | source)
XLA Modules:
  0.0 333.4 jit_solution(12885704497579311177)
XLA Ops:
  7.2 0.0 copy-start
  7.2 0.0 all-gather.6.cloned.1.call-start
  7.2 0.8 add_select_fusion
  8.1 0.4 copy-done
  8.4 0.4 convolution_convert_fusion.2
  8.8 2.2 collective-permute-start.2
  10.9 1.2 collective-permute-start.1
  12.2 2.9 collective-permute-start
  15.1 3.9 %collective-permute-done.2 = bf16[512,256]{1,0:T(8,128)(2,1)S(1)} collective-permute-done((bf16[512,256]{1,0:T(8,128)(2,1)S(1)}, bf16[512,256]{1,0:T(8,128)(2,1)S(1)}, u32[]{:S(2)}, u32[]{:S(2)}) %collective-permute-start.2) | collective-permute-done | bytes 262176 | tf_op jit(solution)/shard_map/ppermute | solution.py:17
  19.0 6.3 %collective-permute-done.1 = bf16[512,256]{1,0:T(8,128)(2,1)S(1)} collective-permute-done((bf16[512,256]{1,0:T(8,128)(2,1)S(1)}, bf16[512,256]{1,0:T(8,128)(2,1)S(1)}, u32[]{:S(2)}, u32[]{:S(2)}) %collective-permute-start.1) | collective-permute-done | bytes 262176 | tf_op jit(solution)/shard_map/ppermute | solution.py:17
  25.3 0.0 collective-permute-done
  25.3 1.0 pad_maximum_fusion
  26.3 0.0 all-gather.6.cloned.1.call-update
  26.4 0.0 reduce-scatter.4.cloned.1.call-start
  26.4 0.7 reshape.49.refs_1_.row_ref
  27.1 0.6 reshape.50.refs_2_.col_ref
  27.7 1.9 fusion.2
  29.6 7.6 %shard_map.103.refs_5_ = f32[16,128,256]{2,1,0:T(8,128)} custom-call(s32[4]{0:T(128)} %bitcast.41, s32[384]{0:T(512)} %reshape.49.refs_1_.row_ref, s32[384]{0:T(512)} %reshape.50.refs_2_.col_ref, bf16[4,96,128,128]{3,2,1,0:T(8,128)(2,1)} %bitcast.27, bf16[4,1,4,128,256]{4,3,2,1,0:T(8,128)(2,1)} %bitcast.37), custom_call_target="tpu_custom_call" | custom-call | tf_op jit(solution)/shard_map/pallas_call | solution.py:133
  37.2 18.0 %all-gather.6.cloned.1.call-done = bf16[12,512,256]{2,1,0:T(8,128)(2,1)} async-done(((bf16[3,512,256]{2,1,0:T(8,128)(2,1)}), bf16[12,512,256]{2,1,0:T(8,128)(2,1)}) %all-gather.6.cloned.1.call-update) | async-done | bytes 3145744 | tf_op jit(solution)/shard_map/all_gather | solution.py:168
  55.2 13.3 %shard_map.104 = bf16[16,128,256]{2,1,0:T(8,128)(2,1)} custom-call(s32[4]{0:T(128)} %bitcast.42, s32[384]{0:T(512)} %reshape.49.refs_1_.row_ref, s32[384]{0:T(512)} %reshape.50.refs_2_.col_ref, bf16[4,96,128,128]{3,2,1,0:T(8,128)(2,1)} %bitcast.28, bf16[4,3,4,128,256]{4,3,2,1,0:T(8,128)(2,1)} %bitcast.36, f32[16,128,256]{2,1,0:T(8,128)} %shard_map.103.refs_5_), custom_call_target="tpu_custom_call" | custom-call | tf_op jit(solution)/shard_map/pallas_call | solution.py:133
  68.5 0.0 reduce-scatter.4.cloned.1.call-update
  68.5 0.0 all-gather.4.cloned.1.call-start
  68.6 24.3 %reduce-scatter.4.cloned.1.call-done = bf16[512,256]{1,0:T(8,128)(2,1)} async-done(((bf16[2048,256]{1,0:T(8,128)(2,1)}), bf16[512,256]{1,0:T(8,128)(2,1)}) %reduce-scatter.4.cloned.1.call-update) | async-done | bytes 262160 | tf_op jit(solution)/shard_map/reduce_scatter | solution.py:190
  92.8 2.1 multiply_convert_fusion
  94.9 1.0 convolution_convert_fusion.1
  95.8 0.0 all-gather.4.cloned.1.call-update
  95.9 0.0 reduce-scatter.8.cloned.1.call-start
  95.9 17.4 %all-gather.4.cloned.1.call-done = bf16[2048,256]{1,0:T(8,128)(2,1)} async-done(((bf16[512,256]{1,0:T(8,128)(2,1)}), bf16[2048,256]{1,0:T(8,128)(2,1)}) %all-gather.4.cloned.1.call-update) | async-done | bytes 1048592 | tf_op jit(solution)/shard_map/all_gather | solution.py:202
  113.3 13.7 %shard_map.106 = bf16[4,3,4,128,256]{4,3,2,1,0:T(8,128)(2,1)} custom-call(s32[4]{0:T(128)} %bitcast.43, s32[384]{0:T(512)} %reshape.49.refs_1_.row_ref, s32[384]{0:T(512)} %reshape.50.refs_2_.col_ref, bf16[4,96,128,128]{3,2,1,0:T(8,128)(2,1)} %bitcast.29, bf16[16,128,256]{2,1,0:T(8,128)(2,1)} %bitcast.32), custom_call_target="tpu_custom_call" | custom-call | tf_op jit(solution)/shard_map/pallas_call | solution.py:133
  127.0 0.0 reduce-scatter.8.cloned.1.call-update
  127.1 0.0 all-reduce.2.cloned.1.call-start
  127.1 0.9 copy-done.1
  128.0 1.0 fusion.8
  128.9 0.0 all-reduce.2.cloned.1.call-update
  129.0 0.0 reduce-scatter.6.cloned.1.call-start
  129.0 7.5 %shard_map.105 = bf16[4,1,4,128,256]{4,3,2,1,0:T(8,128)(2,1)} custom-call(s32[4]{0:T(128)} %bitcast.44, s32[384]{0:T(512)} %reshape.49.refs_1_.row_ref, s32[384]{0:T(512)} %reshape.50.refs_2_.col_ref, bf16[4,96,128,128]{3,2,1,0:T(8,128)(2,1)} %bitcast.30, bf16[16,128,256]{2,1,0:T(8,128)(2,1)} %bitcast.33), custom_call_target="tpu_custom_call" | custom-call | tf_op jit(solution)/shard_map/pallas_call | solution.py:133
  136.5 0.0 reduce-scatter.6.cloned.1.call-update
  136.5 28.1 %reduce-scatter.8.cloned.1.call-done = bf16[1,1536,256]{2,1,0:T(8,128)(2,1)} async-done(((bf16[4,1536,256]{2,1,0:T(8,128)(2,1)}), bf16[1,1536,256]{2,1,0:T(8,128)(2,1)}) %reduce-scatter.8.cloned.1.call-update) | async-done | bytes 786448 | tf_op jit(solution)/shard_map/reduce_scatter | solution.py:217
  164.6 1.2 slice_bitcast_fusion.2
  165.8 1.2 collective-permute-start.3
  167.0 3.0 collective-permute-start.5
  170.1 1.2 collective-permute-start.4
  171.2 126.2 %all-reduce.2.cloned.1.call-done = f32[256,256]{1,0:T(8,128)} async-done(((f32[256,256]{1,0:T(8,128)}), f32[256,256]{1,0:T(8,128)}) %all-reduce.2.cloned.1.call-update) | async-done | bytes 262160 | tf_op jit(solution)/shard_map/psum | solution.py:207
  297.4 1.7 broadcast_multiply_fusion
  299.1 25.2 %reduce-scatter.6.cloned.1.call-done = bf16[512,256]{1,0:T(8,128)(2,1)} async-done(((bf16[2048,256]{1,0:T(8,128)(2,1)}), bf16[512,256]{1,0:T(8,128)(2,1)}) %reduce-scatter.6.cloned.1.call-update) | async-done | bytes 262160 | tf_op jit(solution)/shard_map/reduce_scatter | solution.py:218
  324.3 0.0 collective-permute-done.3
  324.3 0.0 collective-permute-done.5
  324.3 2.3 convolution_convert_fusion
  (12 shorter events, 0.0 us)
Async XLA Ops:
  7.2 1.2 copy-start
  7.2 19.2 %copy-start.3 = (s32[1,1,4,96]{3,2,1,0:T(4,128)S(1)}, s32[1,1,4,96]{3,2,1,0:T(4,128)}, u32[]{:S(2)}) copy-start(s32[1,1,4,96]{3,2,1,0:T(4,128)} %param.10) | copy-start | bytes 4612
  7.2 19.9 %copy-start.4 = (s32[1,1,4,96]{3,2,1,0:T(4,128)S(1)}, s32[1,1,4,96]{3,2,1,0:T(4,128)}, u32[]{:S(2)}) copy-start(s32[1,1,4,96]{3,2,1,0:T(4,128)} %param.11) | copy-start | bytes 4612
  7.2 48.0 %all-gather.6.cloned.1.call-start = ((), (), s32[]{:S(2)}) async-start(), calls=%async_computation.8 | async-start | bytes 3932160 | tf_op jit(solution)/shard_map/all_gather | solution.py:168
  8.8 10.2 %collective-permute-start.2 = (bf16[512,256]{1,0:T(8,128)(2,1)S(1)}, bf16[512,256]{1,0:T(8,128)(2,1)S(1)}, u32[]{:S(2)}, u32[]{:S(2)}) collective-permute-start(bf16[512,256]{1,0:T(8,128)(2,1)S(1)} %convolution_convert_fusion.2), channel_id=1, source_target_pairs={{24,0},{28,4},{0,8},{4,12},{8,16},{12,20},{16,24},{20,28},{25,1},{... | collective-permute-start | bytes 786440 | tf_op jit(solution)/shard_map/ppermute | solution.py:17
  10.9 14.4 %collective-permute-start.1 = (bf16[512,256]{1,0:T(8,128)(2,1)S(1)}, bf16[512,256]{1,0:T(8,128)(2,1)S(1)}, u32[]{:S(2)}, u32[]{:S(2)}) collective-permute-start(bf16[512,256]{1,0:T(8,128)(2,1)S(1)} %convolution_convert_fusion.2), channel_id=1, source_target_pairs={{28,0},{0,4},{4,8},{8,12},{12,16},{16,20},{20,24},{24,28},{29,1},{... | collective-permute-start | bytes 786440 | tf_op jit(solution)/shard_map/ppermute | solution.py:17
  12.2 13.1 %collective-permute-start = (bf16[512,256]{1,0:T(8,128)(2,1)S(1)}, bf16[512,256]{1,0:T(8,128)(2,1)S(1)}, u32[]{:S(2)}, u32[]{:S(2)}) collective-permute-start(bf16[512,256]{1,0:T(8,128)(2,1)S(1)} %convolution_convert_fusion.2), channel_id=1, source_target_pairs={{4,0},{8,4},{12,8},{16,12},{20,16},{24,20},{28,24},{0,28},{5,1},{9... | collective-permute-start | bytes 786440 | tf_op jit(solution)/shard_map/ppermute | solution.py:17
  26.4 66.4 %reduce-scatter.4.cloned.1.call-start = ((), (), s32[]{:S(2)}) async-start(), calls=%async_computation.3 | async-start | bytes 1310720 | tf_op jit(solution)/shard_map/reduce_scatter | solution.py:190
  55.2 37.6 %copy-start.2 = (bf16[256,256]{1,0:T(8,128)(2,1)S(1)}, bf16[256,256]{1,0:T(8,128)(2,1)}, u32[]{:S(2)}) copy-start(bf16[256,256]{1,0:T(8,128)(2,1)} %param.14) | copy-start | bytes 393220
  55.2 37.6 %copy-start.5 = (bf16[512,256]{1,0:T(8,128)(2,1)S(1)}, bf16[512,256]{1,0:T(8,128)(2,1)}, u32[]{:S(2)}) copy-start(bf16[512,256]{1,0:T(8,128)(2,1)} %param.15) | copy-start | bytes 786436
  68.5 44.8 %all-gather.4.cloned.1.call-start = ((), (), s32[]{:S(2)}) async-start(), calls=%async_computation.4 | async-start | bytes 1310720 | tf_op jit(solution)/shard_map/all_gather | solution.py:202
  95.9 68.7 %reduce-scatter.8.cloned.1.call-start = ((), (), s32[]{:S(2)}) async-start(), calls=%async_computation.6 | async-start | bytes 3932160 | tf_op jit(solution)/shard_map/reduce_scatter | solution.py:217
  127.0 1.0 copy-start.1
  127.1 170.4 %all-reduce.2.cloned.1.call-start = ((), (), s32[]{:S(2)}) async-start(), calls=%async_computation.7 | async-start | bytes 524288 | tf_op jit(solution)/shard_map/psum | solution.py:207
  129.0 195.3 %reduce-scatter.6.cloned.1.call-start = ((), (), s32[]{:S(2)}) async-start(), calls=%async_computation.5 | async-start | bytes 1310720 | tf_op jit(solution)/shard_map/reduce_scatter | solution.py:218
  165.8 158.5 %collective-permute-start.3 = (bf16[512,256]{1,0:T(8,128)(2,1)S(1)}, bf16[512,256]{1,0:T(8,128)(2,1)S(1)}, u32[]{:S(2)}, u32[]{:S(2)}) collective-permute-start(bf16[512,256]{1,0:T(8,128)(2,1)S(1)} %get-tuple-element.3), channel_id=1, source_target_pairs={{28,0},{0,4},{4,8},{8,12},{12,16},{16,20},{20,24},{24,28},{29,1},{... | collective-permute-start | bytes 786440 | tf_op jit(solution)/shard_map/ppermute | solution.py:17
  167.0 157.3 %collective-permute-start.5 = (bf16[512,256]{1,0:T(8,128)(2,1)S(1)}, bf16[512,256]{1,0:T(8,128)(2,1)S(1)}, u32[]{:S(2)}, u32[]{:S(2)}) collective-permute-start(bf16[512,256]{1,0:T(8,128)(2,1)S(1)} %get-tuple-element.4), channel_id=1, source_target_pairs={{8,0},{12,4},{16,8},{20,12},{24,16},{28,20},{0,24},{4,28},{9,1},{1... | collective-permute-start | bytes 786440 | tf_op jit(solution)/shard_map/ppermute | solution.py:17
  170.1 154.2 %collective-permute-start.4 = (bf16[512,256]{1,0:T(8,128)(2,1)S(1)}, bf16[512,256]{1,0:T(8,128)(2,1)S(1)}, u32[]{:S(2)}, u32[]{:S(2)}) collective-permute-start(bf16[512,256]{1,0:T(8,128)(2,1)S(1)} %get-tuple-element.5), channel_id=1, source_target_pairs={{4,0},{8,4},{12,8},{16,12},{20,16},{24,20},{28,24},{0,28},{5,1},{9... | collective-permute-start | bytes 786440 | tf_op jit(solution)/shard_map/ppermute | solution.py:17
Sparse Core Ops, SparseCore 0:
  26.5 28.6 all-gather.5
  68.6 24.1 reduce-scatter.3
  96.0 17.2 all-gather.3
  127.2 37.3 reduce-scatter.7
  170.5 126.8 all-reduce.1
  299.8 24.4 reduce-scatter.5
where the time goes:
time: 334 us; the launch traced here: 333 us
  waiting for transfers between devices  250 us (75%)
  Pallas kernels  42 us (13%)
  between operations  14.2 us (4%)
  starting transfers between devices  12 us (4%)
  matrix products  8.46 us (3%)
  local copies, waits for them, and re-layouts  3.72 us (1%)
  other arithmetic  3.45 us (1%)
    psum x1, waiting for transfers between devices, local(): weight_grad = lax.psum(weight_part, ('node', 'rep')) * grad_scale  126 us
    pallas_call x4, Pallas kernels, tile_call(): pl.pallas_call(kernel, out_shape=jax.ShapeDtypeStruct(out_shape, out_dtyp...  42 us
    reduce_scatter x1, waiting for transfers between devices, local(): lax.psum_scatter(away.reshape(reps, 3 * quarter, feat), 'rep', scatter_di...  28.1 us
    reduce_scatter x1, waiting for transfers between devices, local(): lax.psum_scatter(home.reshape(rows_dev, feat), 'rep', scatter_dimension=0...  25.2 us
    reduce_scatter x1, waiting for transfers between devices, local(): lax.psum_scatter(partial_value.reshape(rows_dev, feat), 'rep', scatter_di...  24.3 us
    all_gather x1, waiting for transfers between devices, local(): gathered = lax.all_gather(halo, 'rep', axis=0)  18 us
    all_gather x1, waiting for transfers between devices, local(): lax.all_gather(back_rows, 'rep', axis=0, tiled=True)  17.4 us
    ppermute x6, starting transfers between devices, from_behind(): lax.ppermute(block, axis, [((i - distance) % n, i) for i in range(n)])  11.8 us
  transfers between devices with their start and end apart: 12, of which 8 were waited for; matrix products, arithmetic and copies ran while one was open for 2% of the time, Pallas kernels for 5%

commit v1 on v0

--- a/solution.py
+++ b/solution.py
@@ -144,6 +144,160 @@
     )(*args)
 
 
+def hop(src, dst, send, recv, axis, target):
+    copy = pltpu.make_async_remote_copy(
+        src_ref=src,
+        dst_ref=dst,
+        send_sem=send,
+        recv_sem=recv,
+        device_id={axis: target},
+        device_id_type=pl.DeviceIdType.MESH,
+    )
+    copy.start()
+    return copy
+
+
+def greet(peers):
+    barrier = pltpu.get_barrier_semaphore()
+    for axis, target in peers:
+        pl.semaphore_signal(
+            barrier, inc=1, device_id={axis: target}, device_id_type=pl.DeviceIdType.MESH
+        )
+    pl.semaphore_wait(barrier, len(peers))
+
+
+def dense_kernel(part, cot, weight, act, wpart, back, near, outgoing, far, full, send, recv):
+    me = lax.axis_index("rep")
+    x, c = me // 2, me % 2
+    ox, oc = 1 - x, 1 - c
+    sib, across, diag = x * 2 + oc, ox * 2 + c, ox * 2 + oc
+    greet([("rep", sib), ("rep", across)])
+    first = hop(part.at[diag], near.at[0], send.at[0], recv.at[0], "rep", sib)
+    second = hop(part.at[sib], near.at[1], send.at[1], recv.at[1], "rep", sib)
+    first.wait()
+    outgoing[...] = (part[across].astype(jnp.float32) + near[0].astype(jnp.float32)).astype(
+        outgoing.dtype
+    )
+    third = hop(outgoing, far, send.at[2], recv.at[2], "rep", across)
+    second.wait()
+    mine = part[me].astype(jnp.float32) + near[1].astype(jnp.float32)
+    third.wait()
+    aggregate = (mine + far[...].astype(jnp.float32)).astype(jnp.bfloat16)
+    pre_act = jnp.dot(aggregate, weight[...], preferred_element_type=jnp.float32)
+    gate = jax.nn.sigmoid(pre_act)
+    act[...] = (pre_act * gate).astype(act.dtype)
+    pre_grad = (
+        cot[...].astype(jnp.float32) * gate * (1.0 + pre_act * (1.0 - gate))
+    ).astype(jnp.bfloat16)
+    full[me] = lax.dot_general(
+        pre_grad, weight[...], (((1,), (1,)), ((), ())), preferred_element_type=jnp.float32
+    ).astype(full.dtype)
+    over = hop(full.at[me], full.at[me], send.at[3], recv.at[3], "rep", across)
+    side = hop(full.at[me], full.at[me], send.at[4], recv.at[4], "rep", sib)
+    wpart[...] = lax.dot_general(
+        aggregate, pre_grad, (((0,), (0,)), ((), ())), preferred_element_type=jnp.float32
+    )
+    over.wait()
+    relay = hop(full.at[across], full.at[across], send.at[5], recv.at[5], "rep", sib)
+    side.wait()
+    relay.wait()
+    back[...] = full[...]
+
+
+def sum_kernel(nodes, reps, scale, part, out, from_rep, held, from_node, full, rs, rr, ns, nr, gs, gr, os, orr):
+    me, here = lax.axis_index("rep"), lax.axis_index("node")
+    rep_peers = [(me + d) % reps for d in range(1, reps)]
+    node_peers = [(here + d) % nodes for d in range(1, nodes)]
+    greet([("rep", p) for p in rep_peers] + [("node", p) for p in node_peers])
+    copies = [
+        hop(part.at[p], from_rep.at[i], rs.at[i], rr.at[i], "rep", p)
+        for i, p in enumerate(rep_peers)
+    ]
+    for copy in copies:
+        copy.wait()
+    total = part[me]
+    for i in range(reps - 1):
+        total = total + from_rep[i]
+    held[...] = total
+    copies = [
+        hop(held.at[p], from_node.at[i], ns.at[i], nr.at[i], "node", p)
+        for i, p in enumerate(node_peers)
+    ]
+    for copy in copies:
+        copy.wait()
+    total = held[here]
+    for i in range(nodes - 1):
+        total = total + from_node[i]
+    full[me, here] = total * scale
+    copies = [
+        hop(full.at[me, here], full.at[me, here], gs.at[i], gr.at[i], "node", p)
+        for i, p in enumerate(node_peers)
+    ]
+    for copy in copies:
+        copy.wait()
+    copies = [
+        hop(full.at[me], full.at[me], os.at[i], orr.at[i], "rep", p)
+        for i, p in enumerate(rep_peers)
+    ]
+    for copy in copies:
+        copy.wait()
+    out[...] = full[...]
+
+
+def comm_params(ident):
+    return pltpu.CompilerParams(
+        collective_id=ident, has_side_effects=True, vmem_limit_bytes=60 * 1024 * 1024
+    )
+
+
+def dense_call(part, cot, weight):
+    reps, rows, feat = part.shape
+    vmem = pl.BlockSpec(memory_space=pltpu.VMEM)
+    half = (rows, feat)
+    return pl.pallas_call(
+        dense_kernel,
+        out_shape=(
+            jax.ShapeDtypeStruct(half, jnp.bfloat16),
+            jax.ShapeDtypeStruct((feat, feat), jnp.float32),
+            jax.ShapeDtypeStruct(part.shape, jnp.bfloat16),
+        ),
+        in_specs=[vmem] * 3,
+        out_specs=(vmem,) * 3,
+        scratch_shapes=[
+            pltpu.VMEM((2,) + half, jnp.bfloat16),
+            pltpu.VMEM(half, jnp.bfloat16),
+            pltpu.VMEM(half, jnp.bfloat16),
+            pltpu.VMEM(part.shape, jnp.bfloat16),
+            pltpu.SemaphoreType.DMA((6,)),
+            pltpu.SemaphoreType.DMA((6,)),
+        ],
+        compiler_params=comm_params(0),
+    )(part, cot, weight)
+
+
+def sum_call(part, scale):
+    nodes, reps = lax.axis_size("node"), lax.axis_size("rep")
+    rows = part.size // (nodes * reps * 128)
+    shape = (reps, nodes, rows, 128)
+    vmem = pl.BlockSpec(memory_space=pltpu.VMEM)
+    sems = [pltpu.SemaphoreType.DMA((n - 1,)) for n in (reps, reps, nodes, nodes, nodes, nodes, reps, reps)]
+    out = pl.pallas_call(
+        functools.partial(sum_kernel, nodes, reps, scale),
+        out_shape=jax.ShapeDtypeStruct(shape, jnp.float32),
+        in_specs=[vmem],
+        out_specs=vmem,
+        scratch_shapes=[
+            pltpu.VMEM((reps - 1, nodes, rows, 128), jnp.float32),
+            pltpu.VMEM((nodes, rows, 128), jnp.float32),
+            pltpu.VMEM((nodes - 1, rows, 128), jnp.float32),
+            pltpu.VMEM(shape, jnp.float32),
+        ]
+        + sems,
+        compiler_params=comm_params(1),
+    )(part.reshape(shape))
+    return out.reshape(part.shape)
+
+
 def local(features, tiles, tile_rows, tile_cols, tile_count, order, weight, cotangent):
     rows_dev, feat = features.shape
     size = tiles.shape[-1]
@@ -187,24 +341,12 @@
         functools.partial(forward_kernel, (0, 2, 3), capacity, True),
         (0, 2, 3), acc_shape, jnp.bfloat16, acc_shape, scalars + (gathered, own), tile_set,
     )
-    aggregate = lax.psum_scatter(
-        partial_value.reshape(rows_dev, feat), "rep", scatter_dimension=0, tiled=True
-    )
-    pre_act = jnp.dot(aggregate, weight, preferred_element_type=jnp.float32)
-    gate_val = jax.nn.sigmoid(pre_act)
-    activated = (pre_act * gate_val).astype(jnp.bfloat16)
-    pre_grad = (
-        cotangent.astype(jnp.float32) * gate_val * (1.0 + pre_act * (1.0 - gate_val))
-    ).astype(jnp.bfloat16)
-    back_rows = lax.dot_general(
-        pre_grad, weight, (((1,), (1,)), ((), ())), preferred_element_type=jnp.float32
-    ).astype(jnp.bfloat16)
-    full_back = lax.all_gather(back_rows, "rep", axis=0, tiled=True).reshape(blocks, size, feat)
-    weight_part = lax.dot_general(
-        aggregate, pre_grad, (((0,), (0,)), ((), ())), preferred_element_type=jnp.float32
-    )
+    activated, weight_part, full_back = dense_call(
+        partial_value.reshape(reps, quarter, feat), cotangent, weight
+    )
+    full_back = full_back.reshape(blocks, size, feat)
     grad_scale = 1.0 / math.sqrt(rows_dev * lax.axis_size("node"))
-    weight_grad = lax.psum(weight_part, ("node", "rep")) * grad_scale
+    weight_grad = sum_call(weight_part, grad_scale)
 
     away = tile_call(
         functools.partial(backward_kernel, (0, 2, 3), capacity),

time: 334 us -> 183 us (0.55)
  waiting for transfers between devices: 250 us -> 63.7 us
  Pallas kernels: 42 us -> 81.4 us
  matrix products: 8.46 us -> 4.49 us
    psum x1 -> x0, waiting for transfers between devices: 126 us -> none  [local(): weight_grad = lax.psum(weight_part, ('node', 'rep')) * grad_scale]
    pallas_call x0 -> x2, Pallas kernels: none -> 44.3 us  [the longest x1 22.9 us: sum_call(): pl.pallas_call(functools.partial(sum_kernel, nodes, reps, scale), out_sha...]
    reduce_scatter x1, waiting for transfers between devices: 25.2 us -> 0.01 us  [local(): lax.psum_scatter(home.reshape(rows_dev, feat), 'rep', scatter_dimension=0...]
    reduce_scatter x1 -> x0, waiting for transfers between devices: 24.3 us -> none  [local(): lax.psum_scatter(partial_value.reshape(rows_dev, feat), 'rep', scatter_di...]
    all_gather x1 -> x0, waiting for transfers between devices: 17.4 us -> none  [local(): lax.all_gather(back_rows, 'rep', axis=0, tiled=True)]
    reduce_scatter x1, waiting for transfers between devices: 28.1 us -> 35.4 us  [local(): lax.psum_scatter(away.reshape(reps, 3 * quarter, feat), 'rep', scatter_di...]
    pallas_call x4, Pallas kernels: 42 us -> 37.1 us  [tile_call(): pl.pallas_call(kernel, out_shape=jax.ShapeDtypeStruct(out_shape, out_dtyp...]
    dot_general x3 -> x0, matrix products: 3.99 us -> none  [the longest x1 2.06 us: local(): pre_act = jnp.dot(aggregate, weight, preferred_element_type=jnp.float32)]
  transfers between devices with their start and end apart: 12 -> 9, of which waited for: 8 -> 4; matrix products, arithmetic and copies ran while one was open for 2% -> 4% of each run, Pallas kernels for 5% -> 21%
where the time goes in v1:
time: 183 us
  Pallas kernels  81.4 us (44%)
  waiting for transfers between devices  63.7 us (35%)
  between operations  13.9 us (8%)
  starting transfers between devices  11.9 us (7%)
  local copies, waits for them, and re-layouts  6.03 us (3%)
  matrix products  4.49 us (2%)
    pallas_call x4, Pallas kernels, tile_call(): pl.pallas_call(kernel, out_shape=jax.ShapeDtypeStruct(out_shape, out_dtyp...  37.1 us
    reduce_scatter x1, waiting for transfers between devices, local(): lax.psum_scatter(away.reshape(reps, 3 * quarter, feat), 'rep', scatter_di...  35.4 us
    pallas_call x1, Pallas kernels, sum_call(): pl.pallas_call(functools.partial(sum_kernel, nodes, reps, scale), out_sha...  22.9 us
    pallas_call x1, Pallas kernels, dense_call(): pl.pallas_call(dense_kernel, out_shape=(jax.ShapeDtypeStruct(half, jnp.bf...  21.4 us
    all_gather x1, waiting for transfers between devices, local(): gathered = lax.all_gather(halo, 'rep', axis=0)  18 us
    ppermute x6, starting transfers between devices, from_behind(): lax.ppermute(block, axis, [((i - distance) % n, i) for i in range(n)])  11.8 us
    ppermute x6, waiting for transfers between devices, from_behind(): lax.ppermute(block, axis, [((i - distance) % n, i) for i in range(n)])  10.2 us
  transfers between devices with their start and end apart: 9, of which 4 were waited for; matrix products, arithmetic and copies ran while one was open for 4% of the time, Pallas kernels for 21%

profile of v1, /device:TPU:1, one launch (start us, length us, event | category | flops | bytes accessed | tf_op | source)
XLA Modules:
  0.0 183.2 jit_solution(8480212857837139503)
XLA Ops:
  7.2 0.0 copy-start
  7.2 0.0 copy-start.3
  7.2 0.0 copy-start.4
  7.2 0.0 all-gather.3.cloned.1.call-start
  7.2 0.8 add_select_fusion
  8.1 0.4 copy-done
  8.4 0.4 convolution_convert_fusion.1
  8.8 2.2 %collective-permute-start.2 = (bf16[512,256]{1,0:T(8,128)(2,1)S(1)}, bf16[512,256]{1,0:T(8,128)(2,1)S(1)}, u32[]{:S(2)}, u32[]{:S(2)}) collective-permute-start(bf16[512,256]{1,0:T(8,128)(2,1)S(1)} %convolution_convert_fusion.1), channel_id=1, source_target_pairs={{24,0},{28,4},{0,8},{4,12},{8,16},{12,20},{16,24},{20,28},{25,1},{... | collective-permute-start | bytes 786440 | tf_op jit(solution)/shard_map/ppermute | solution.py:17
  10.9 1.2 collective-permute-start.1
  12.2 2.9 %collective-permute-start = (bf16[512,256]{1,0:T(8,128)(2,1)S(1)}, bf16[512,256]{1,0:T(8,128)(2,1)S(1)}, u32[]{:S(2)}, u32[]{:S(2)}) collective-permute-start(bf16[512,256]{1,0:T(8,128)(2,1)S(1)} %convolution_convert_fusion.1), channel_id=1, source_target_pairs={{4,0},{8,4},{12,8},{16,12},{20,16},{24,20},{28,24},{0,28},{5,1},{9... | collective-permute-start | bytes 786440 | tf_op jit(solution)/shard_map/ppermute | solution.py:17
  15.1 3.9 %collective-permute-done.2 = bf16[512,256]{1,0:T(8,128)(2,1)S(1)} collective-permute-done((bf16[512,256]{1,0:T(8,128)(2,1)S(1)}, bf16[512,256]{1,0:T(8,128)(2,1)S(1)}, u32[]{:S(2)}, u32[]{:S(2)}) %collective-permute-start.2) | collective-permute-done | bytes 262176 | tf_op jit(solution)/shard_map/ppermute | solution.py:17
  19.0 6.3 %collective-permute-done.1 = bf16[512,256]{1,0:T(8,128)(2,1)S(1)} collective-permute-done((bf16[512,256]{1,0:T(8,128)(2,1)S(1)}, bf16[512,256]{1,0:T(8,128)(2,1)S(1)}, u32[]{:S(2)}, u32[]{:S(2)}) %collective-permute-start.1) | collective-permute-done | bytes 262176 | tf_op jit(solution)/shard_map/ppermute | solution.py:17
  25.3 0.0 collective-permute-done
  25.3 1.0 pad_maximum_fusion
  26.3 0.0 all-gather.3.cloned.1.call-update
  26.4 0.0 reduce-scatter.5.cloned.1.call-start
  26.4 0.0 copy-done.3
  26.4 0.7 reshape.55.refs_1_.row_ref
  27.1 0.0 copy-done.4
  27.1 0.7 reshape.56.refs_2_.col_ref
  27.7 1.9 %fusion.2 = bf16[4,512,256]{2,1,0:T(8,128)(2,1)} fusion(bf16[4,512,256]{2,1,0:T(8,128)(2,1)S(1)} %bitcast.22, s32[4,512]{1,0:T(4,128)S(1)} %reshape.57), kind=kOutput, calls=%fused_computation.3 | convolution fusion | flops 538443776 | bytes 2105344 | tf_op jit(solution)/shard_map/qpi,qif->qpf/dot_general | solution.py:326
  29.6 7.6 %shard_map.103.refs_5_ = f32[16,128,256]{2,1,0:T(8,128)} custom-call(s32[4]{0:T(128)} %bitcast.37, s32[384]{0:T(512)} %reshape.55.refs_1_.row_ref, s32[384]{0:T(512)} %reshape.56.refs_2_.col_ref, bf16[4,96,128,128]{3,2,1,0:T(8,128)(2,1)} %bitcast.23, bf16[4,1,4,128,256]{4,3,2,1,0:T(8,128)(2,1)} %bitcast.33), custom_call_target="tpu_custom_call" | custom-call | tf_op jit(solution)/shard_map/pallas_call | solution.py:133
  37.2 18.0 %all-gather.3.cloned.1.call-done = bf16[12,512,256]{2,1,0:T(8,128)(2,1)} async-done(((bf16[3,512,256]{2,1,0:T(8,128)(2,1)}), bf16[12,512,256]{2,1,0:T(8,128)(2,1)}) %all-gather.3.cloned.1.call-update) | async-done | bytes 3145744 | tf_op jit(solution)/shard_map/all_gather | solution.py:322
  55.2 10.8 %shard_map.104 = bf16[16,128,256]{2,1,0:T(8,128)(2,1)} custom-call(s32[4]{0:T(128)} %bitcast.38, s32[384]{0:T(512)} %reshape.55.refs_1_.row_ref, s32[384]{0:T(512)} %reshape.56.refs_2_.col_ref, bf16[4,96,128,128]{3,2,1,0:T(8,128)(2,1)} %bitcast.24, bf16[4,3,4,128,256]{4,3,2,1,0:T(8,128)(2,1)} %bitcast.32, f32[16,128,256]{2,1,0:T(8,128)} %shard_map.103.refs_5_), custom_call_target="tpu_custom_call" | custom-call | tf_op jit(solution)/shard_map/pallas_call | solution.py:133
  66.0 21.4 %shard_map.105 = (bf16[512,256]{1,0:T(8,128)(2,1)}, f32[256,256]{1,0:T(8,128)}, bf16[4,512,256]{2,1,0:T(8,128)(2,1)}) custom-call(bf16[4,512,256]{2,1,0:T(8,128)(2,1)} %bitcast.31, bf16[512,256]{1,0:T(8,128)(2,1)} %cot.1, bf16[256,256]{1,0:T(8,128)(2,1)} %weight.1), custom_call_target="tpu_custom_call" | custom-call | tf_op jit(solution)/shard_map/pallas_call | solution.py:257
  87.4 11.2 %shard_map.107 = bf16[4,3,4,128,256]{4,3,2,1,0:T(8,128)(2,1)} custom-call(s32[4]{0:T(128)} %bitcast.39, s32[384]{0:T(512)} %reshape.55.refs_1_.row_ref, s32[384]{0:T(512)} %reshape.56.refs_2_.col_ref, bf16[4,96,128,128]{3,2,1,0:T(8,128)(2,1)} %bitcast.25, bf16[16,128,256]{2,1,0:T(8,128)(2,1)} %bitcast.28), custom_call_target="tpu_custom_call" | custom-call | tf_op jit(solution)/shard_map/pallas_call | solution.py:133
  98.6 0.0 reduce-scatter.5.cloned.1.call-update
  98.6 0.0 copy-start.2
  98.6 0.0 reduce-scatter.3.cloned.1.call-start
  98.6 7.5 %shard_map.106 = bf16[4,1,4,128,256]{4,3,2,1,0:T(8,128)(2,1)} custom-call(s32[4]{0:T(128)} %bitcast.40, s32[384]{0:T(512)} %reshape.55.refs_1_.row_ref, s32[384]{0:T(512)} %reshape.56.refs_2_.col_ref, bf16[4,96,128,128]{3,2,1,0:T(8,128)(2,1)} %bitcast.26, bf16[16,128,256]{2,1,0:T(8,128)(2,1)} %bitcast.29), custom_call_target="tpu_custom_call" | custom-call | tf_op jit(solution)/shard_map/pallas_call | solution.py:133
  106.2 0.0 copy-start.1
  106.2 0.0 reduce-scatter.3.cloned.1.call-update
  106.2 35.4 %reduce-scatter.5.cloned.1.call-done = bf16[1,1536,256]{2,1,0:T(8,128)(2,1)} async-done(((bf16[4,1536,256]{2,1,0:T(8,128)(2,1)}), bf16[1,1536,256]{2,1,0:T(8,128)(2,1)}) %reduce-scatter.5.cloned.1.call-update) | async-done | bytes 786448 | tf_op jit(solution)/shard_map/reduce_scatter | solution.py:359
  141.6 1.2 slice_bitcast_fusion.2
  142.8 1.3 collective-permute-start.3
  144.1 3.1 %collective-permute-start.5 = (bf16[512,256]{1,0:T(8,128)(2,1)S(1)}, bf16[512,256]{1,0:T(8,128)(2,1)S(1)}, u32[]{:S(2)}, u32[]{:S(2)}) collective-permute-start(bf16[512,256]{1,0:T(8,128)(2,1)S(1)} %get-tuple-element.10), channel_id=1, source_target_pairs={{8,0},{12,4},{16,8},{20,12},{24,16},{28,20},{0,24},{4,28},{9,1},{1... | collective-permute-start | bytes 786440 | tf_op jit(solution)/shard_map/ppermute | solution.py:17
  147.1 1.2 collective-permute-start.4
  148.3 0.0 copy-done.2
  148.3 0.7 reshape.65.part
  149.0 22.9 %shard_map.108 = f32[4,8,16,128]{3,2,1,0:T(8,128)} custom-call(f32[4,8,16,128]{3,2,1,0:T(8,128)} %reshape.65.part), custom_call_target="tpu_custom_call" | custom-call | tf_op jit(solution)/shard_map/pallas_call | solution.py:284
  172.0 1.7 reshape.66
  173.7 0.0 reduce-scatter.3.cloned.1.call-done
  173.7 0.0 collective-permute-done.3
  173.7 0.0 collective-permute-done.5
  173.7 0.0 collective-permute-done.4
  173.7 2.3 %convolution_convert_fusion = bf16[512,256]{1,0:T(8,128)(2,1)} fusion(s32[512]{0:T(512)S(1)} %bitcast.42, bf16[512,256]{1,0:T(8,128)(2,1)S(1)} %collective-permute-done.5, bf16[512,256]{1,0:T(8,128)(2,1)S(1)} %collective-permute-done.4, bf16[512,256]{1,0:T(8,128)(2,1)S(1)} %collective-permute-done.3, bf16[512,256]{1,0:T(8,128)(2,1)} %reduce-scatter.3.cloned.1.call-done), kind=kOutput, calls=%fused_computation.4 | convolution fusion | flops 135659520 | bytes 1312768 | tf_op jit(solution)/shard_map/dot_general | solution.py:365
  176.0 0.0 copy-done.1
  176.0 0.7 copy.12
  (2 shorter events, 0.0 us)
Async XLA Ops:
  7.2 1.2 copy-start
  7.2 19.2 %copy-start.3 = (s32[1,1,4,96]{3,2,1,0:T(4,128)S(1)}, s32[1,1,4,96]{3,2,1,0:T(4,128)}, u32[]{:S(2)}) copy-start(s32[1,1,4,96]{3,2,1,0:T(4,128)} %param.10) | copy-start | bytes 4612
  7.2 19.9 %copy-start.4 = (s32[1,1,4,96]{3,2,1,0:T(4,128)S(1)}, s32[1,1,4,96]{3,2,1,0:T(4,128)}, u32[]{:S(2)}) copy-start(s32[1,1,4,96]{3,2,1,0:T(4,128)} %param.11) | copy-start | bytes 4612
  7.2 48.0 %all-gather.3.cloned.1.call-start = ((), (), s32[]{:S(2)}) async-start(), calls=%async_computation.4 | async-start | bytes 3932160 | tf_op jit(solution)/shard_map/all_gather | solution.py:322
  8.8 10.2 %collective-permute-start.2 = (bf16[512,256]{1,0:T(8,128)(2,1)S(1)}, bf16[512,256]{1,0:T(8,128)(2,1)S(1)}, u32[]{:S(2)}, u32[]{:S(2)}) collective-permute-start(bf16[512,256]{1,0:T(8,128)(2,1)S(1)} %convolution_convert_fusion.1), channel_id=1, source_target_pairs={{24,0},{28,4},{0,8},{4,12},{8,16},{12,20},{16,24},{20,28},{25,1},{... | collective-permute-start | bytes 786440 | tf_op jit(solution)/shard_map/ppermute | solution.py:17
  10.9 14.4 %collective-permute-start.1 = (bf16[512,256]{1,0:T(8,128)(2,1)S(1)}, bf16[512,256]{1,0:T(8,128)(2,1)S(1)}, u32[]{:S(2)}, u32[]{:S(2)}) collective-permute-start(bf16[512,256]{1,0:T(8,128)(2,1)S(1)} %convolution_convert_fusion.1), channel_id=1, source_target_pairs={{28,0},{0,4},{4,8},{8,12},{12,16},{16,20},{20,24},{24,28},{29,1},{... | collective-permute-start | bytes 786440 | tf_op jit(solution)/shard_map/ppermute | solution.py:17
  12.2 13.1 %collective-permute-start = (bf16[512,256]{1,0:T(8,128)(2,1)S(1)}, bf16[512,256]{1,0:T(8,128)(2,1)S(1)}, u32[]{:S(2)}, u32[]{:S(2)}) collective-permute-start(bf16[512,256]{1,0:T(8,128)(2,1)S(1)} %convolution_convert_fusion.1), channel_id=1, source_target_pairs={{4,0},{8,4},{12,8},{16,12},{20,16},{24,20},{28,24},{0,28},{5,1},{9... | collective-permute-start | bytes 786440 | tf_op jit(solution)/shard_map/ppermute | solution.py:17
  26.4 115.3 %reduce-scatter.5.cloned.1.call-start = ((), (), s32[]{:S(2)}) async-start(), calls=%async_computation.3 | async-start | bytes 3932160 | tf_op jit(solution)/shard_map/reduce_scatter | solution.py:359
  98.6 49.7 %copy-start.2 = (f32[256,256]{1,0:T(8,128)S(1)}, f32[256,256]{1,0:T(8,128)}, u32[]{:S(2)}) copy-start(f32[256,256]{1,0:T(8,128)} %get-tuple-element.8) | copy-start | bytes 786436
  98.6 75.1 %reduce-scatter.3.cloned.1.call-start = ((), (), s32[]{:S(2)}) async-start(), calls=%async_computation.2 | async-start | bytes 1310720 | tf_op jit(solution)/shard_map/reduce_scatter | solution.py:360
  106.2 69.8 %copy-start.1 = (bf16[512,256]{1,0:T(8,128)(2,1)S(1)}, bf16[512,256]{1,0:T(8,128)(2,1)}, u32[]{:S(2)}) copy-start(bf16[512,256]{1,0:T(8,128)(2,1)} %get-tuple-element.15) | copy-start | bytes 786436
  142.8 30.9 %collective-permute-start.3 = (bf16[512,256]{1,0:T(8,128)(2,1)S(1)}, bf16[512,256]{1,0:T(8,128)(2,1)S(1)}, u32[]{:S(2)}, u32[]{:S(2)}) collective-permute-start(bf16[512,256]{1,0:T(8,128)(2,1)S(1)} %get-tuple-element.9), channel_id=1, source_target_pairs={{28,0},{0,4},{4,8},{8,12},{12,16},{16,20},{20,24},{24,28},{29,1},{... | collective-permute-start | bytes 786440 | tf_op jit(solution)/shard_map/ppermute | solution.py:17
  144.1 29.6 %collective-permute-start.5 = (bf16[512,256]{1,0:T(8,128)(2,1)S(1)}, bf16[512,256]{1,0:T(8,128)(2,1)S(1)}, u32[]{:S(2)}, u32[]{:S(2)}) collective-permute-start(bf16[512,256]{1,0:T(8,128)(2,1)S(1)} %get-tuple-element.10), channel_id=1, source_target_pairs={{8,0},{12,4},{16,8},{20,12},{24,16},{28,20},{0,24},{4,28},{9,1},{1... | collective-permute-start | bytes 786440 | tf_op jit(solution)/shard_map/ppermute | solution.py:17
  147.1 26.6 %collective-permute-start.4 = (bf16[512,256]{1,0:T(8,128)(2,1)S(1)}, bf16[512,256]{1,0:T(8,128)(2,1)S(1)}, u32[]{:S(2)}, u32[]{:S(2)}) collective-permute-start(bf16[512,256]{1,0:T(8,128)(2,1)S(1)} %get-tuple-element.11), channel_id=1, source_target_pairs={{4,0},{8,4},{12,8},{16,12},{20,16},{24,20},{28,24},{0,28},{5,1},{9... | collective-permute-start | bytes 786440 | tf_op jit(solution)/shard_map/ppermute | solution.py:17
Sparse Core Ops, SparseCore 0:
  26.5 28.6 all-gather.2
  98.7 42.8 reduce-scatter.4
  144.2 24.8 reduce-scatter.2

commit v2 on v1

--- a/solution.py
+++ b/solution.py
@@ -10,11 +10,6 @@
 
 CHUNK = 8
 GROUP = 4
-
-
-def from_behind(block, axis, distance):
-    n = lax.axis_size(axis)
-    return lax.ppermute(block, axis, [((i - distance) % n, i) for i in range(n)])
 
 
 def stream(tiles, held, sems, count_ref, ks, step):
@@ -204,44 +199,169 @@
     back[...] = full[...]
 
 
-def sum_kernel(nodes, reps, scale, part, out, from_rep, held, from_node, full, rs, rr, ns, nr, gs, gr, os, orr):
+def halo_kernel(nodes, mine, out, full, send, recv):
     me, here = lax.axis_index("rep"), lax.axis_index("node")
+    x, c = me // 2, me % 2
+    sib, across = x * 2 + 1 - c, (1 - x) * 2 + c
+    greet(
+        [("rep", sib), ("rep", across)]
+        + [("node", (here + d) % nodes) for d in (1, nodes - 1, 2, nodes - 2)]
+    )
+    arrivals = [
+        hop(mine, full.at[me, j], send.at[j], recv.at[j], "node", (here + d) % nodes)
+        for j, d in enumerate((nodes - 1, 1, 2))
+    ]
+    over, rest = [], []
+    for j in range(3):
+        arrivals[j].wait()
+        own = full.at[me, j]
+        over.append(hop(own, own, send.at[3 + j], recv.at[3 + j], "rep", across))
+        rest.append(hop(own, own, send.at[6 + j], recv.at[6 + j], "rep", sib))
+    for j in range(3):
+        over[j].wait()
+        other = full.at[across, j]
+        rest.append(hop(other, other, send.at[9 + j], recv.at[9 + j], "rep", sib))
+    for copy in rest:
+        copy.wait()
+    out[...] = full[...]
+
+
+def halo_call(mine, reps):
+    shape = (reps, 3) + mine.shape
+    vmem = pl.BlockSpec(memory_space=pltpu.VMEM)
+    return pl.pallas_call(
+        functools.partial(halo_kernel, lax.axis_size("node")),
+        out_shape=jax.ShapeDtypeStruct(shape, mine.dtype),
+        in_specs=[vmem],
+        out_specs=vmem,
+        scratch_shapes=[
+            pltpu.VMEM(shape, mine.dtype),
+            pltpu.SemaphoreType.DMA((12,)),
+            pltpu.SemaphoreType.DMA((12,)),
+        ],
+        compiler_params=comm_params(2),
+    )(mine)
+
+
+def finish_kernel(
+    nodes, reps, scale, terms, pick, part, grad, out,
+    near, outgoing, far, leaving, got, total, from_rep, held, from_node, full,
+    send, recv, rs, rr, ns, nr, gs, gr, os, orr,
+):
+    me, here = lax.axis_index("rep"), lax.axis_index("node")
+    x, c = me // 2, me % 2
+    sib, across, diag = x * 2 + 1 - c, (1 - x) * 2 + c, (1 - x) * 2 + 1 - c
     rep_peers = [(me + d) % reps for d in range(1, reps)]
     node_peers = [(here + d) % nodes for d in range(1, nodes)]
     greet([("rep", p) for p in rep_peers] + [("node", p) for p in node_peers])
-    copies = [
+    first = [
+        hop(terms.at[diag, j], near.at[0, j], send.at[j], recv.at[j], "rep", sib)
+        for j in range(4)
+    ]
+    second = [
+        hop(terms.at[sib, j], near.at[1, j], send.at[4 + j], recv.at[4 + j], "rep", sib)
+        for j in range(4)
+    ]
+    to_reps = [
         hop(part.at[p], from_rep.at[i], rs.at[i], rr.at[i], "rep", p)
         for i, p in enumerate(rep_peers)
     ]
-    for copy in copies:
-        copy.wait()
-    total = part[me]
+    third = []
+    for j in range(4):
+        first[j].wait()
+        outgoing[j] = (
+            terms[across, j].astype(jnp.float32) + near[0, j].astype(jnp.float32)
+        ).astype(outgoing.dtype)
+        third.append(hop(outgoing.at[j], far.at[j], send.at[8 + j], recv.at[8 + j], "rep", across))
+    for copy in to_reps:
+        copy.wait()
+    share = part[me]
     for i in range(reps - 1):
-        total = total + from_rep[i]
-    held[...] = total
-    copies = [
+        share = share + from_rep[i]
+    held[...] = share
+    to_nodes = [
         hop(held.at[p], from_node.at[i], ns.at[i], nr.at[i], "node", p)
         for i, p in enumerate(node_peers)
     ]
-    for copy in copies:
-        copy.wait()
-    total = held[here]
+    fourth = []
+    for j, d in enumerate((1, nodes - 1, nodes - 2, 0)):
+        second[j].wait()
+        third[j].wait()
+        value = (
+            terms[me, j].astype(jnp.float32)
+            + near[1, j].astype(jnp.float32)
+            + far[j].astype(jnp.float32)
+        )
+        if d:
+            leaving[j] = value.astype(leaving.dtype)
+            fourth.append(
+                hop(leaving.at[j], got.at[j], send.at[12 + j], recv.at[12 + j], "node", (here + d) % nodes)
+            )
+        else:
+            total[...] = value
+    for copy in to_nodes:
+        copy.wait()
+    share = held[here]
     for i in range(nodes - 1):
-        total = total + from_node[i]
-    full[me, here] = total * scale
-    copies = [
+        share = share + from_node[i]
+    full[me, here] = share * scale
+    spread = [
         hop(full.at[me, here], full.at[me, here], gs.at[i], gr.at[i], "node", p)
         for i, p in enumerate(node_peers)
     ]
-    for copy in copies:
-        copy.wait()
-    copies = [
+    for copy in spread:
+        copy.wait()
+    gather = [
         hop(full.at[me], full.at[me], os.at[i], orr.at[i], "rep", p)
         for i, p in enumerate(rep_peers)
     ]
-    for copy in copies:
+    for copy in fourth:
+        copy.wait()
+    value = total[...]
+    for j in range(3):
+        value = value + got[j].astype(jnp.float32)
+    grad[...] = lax.dot_general(
+        pick[...], value.astype(jnp.bfloat16), (((0,), (0,)), ((), ())), preferred_element_type=jnp.float32
+    ).astype(grad.dtype)
+    for copy in gather:
         copy.wait()
     out[...] = full[...]
+
+
+def finish_call(terms, pick, part, scale):
+    nodes, reps = lax.axis_size("node"), lax.axis_size("rep")
+    rows = part.size // (nodes * reps * 128)
+    shape = (reps, nodes, rows, 128)
+    block = terms.shape[2:]
+    vmem = pl.BlockSpec(memory_space=pltpu.VMEM)
+    sems = [
+        pltpu.SemaphoreType.DMA((n,))
+        for n in (15, 15) + (reps - 1,) * 2 + (nodes - 1,) * 4 + (reps - 1,) * 2
+    ]
+    grad, out = pl.pallas_call(
+        functools.partial(finish_kernel, nodes, reps, scale),
+        out_shape=(
+            jax.ShapeDtypeStruct(block, jnp.bfloat16),
+            jax.ShapeDtypeStruct(shape, jnp.float32),
+        ),
+        in_specs=[vmem] * 3,
+        out_specs=(vmem,) * 2,
+        scratch_shapes=[
+            pltpu.VMEM((2, 4) + block, jnp.bfloat16),
+            pltpu.VMEM((4,) + block, jnp.bfloat16),
+            pltpu.VMEM((4,) + block, jnp.bfloat16),
+            pltpu.VMEM((3,) + block, jnp.bfloat16),
+            pltpu.VMEM((3,) + block, jnp.bfloat16),
+            pltpu.VMEM(block, jnp.float32),
+            pltpu.VMEM((reps - 1, nodes, rows, 128), jnp.float32),
+            pltpu.VMEM((nodes, rows, 128), jnp.float32),
+            pltpu.VMEM((nodes - 1, rows, 128), jnp.float32),
+            pltpu.VMEM(shape, jnp.float32),
+        ]
+        + sems,
+        compiler_params=comm_params(1),
+    )(terms, pick, part.reshape(shape))
+    return grad, out.reshape(part.shape)
 
 
 def comm_params(ident):
@@ -275,29 +395,6 @@
     )(part, cot, weight)
 
 
-def sum_call(part, scale):
-    nodes, reps = lax.axis_size("node"), lax.axis_size("rep")
-    rows = part.size // (nodes * reps * 128)
-    shape = (reps, nodes, rows, 128)
-    vmem = pl.BlockSpec(memory_space=pltpu.VMEM)
-    sems = [pltpu.SemaphoreType.DMA((n - 1,)) for n in (reps, reps, nodes, nodes, nodes, nodes, reps, reps)]
-    out = pl.pallas_call(
-        functools.partial(sum_kernel, nodes, reps, scale),
-        out_shape=jax.ShapeDtypeStruct(shape, jnp.float32),
-        in_specs=[vmem],
-        out_specs=vmem,
-        scratch_shapes=[
-            pltpu.VMEM((reps - 1, nodes, rows, 128), jnp.float32),
-            pltpu.VMEM((nodes, rows, 128), jnp.float32),
-            pltpu.VMEM((nodes - 1, rows, 128), jnp.float32),
-            pltpu.VMEM(shape, jnp.float32),
-        ]
-        + sems,
-        compiler_params=comm_params(1),
-    )(part.reshape(shape))
-    return out.reshape(part.shape)
-
-
 def local(features, tiles, tile_rows, tile_cols, tile_count, order, weight, cotangent):
     rows_dev, feat = features.shape
     size = tiles.shape[-1]
@@ -318,8 +415,7 @@
     my_pick = (my_order[:, None] == spots[None, :]).astype(jnp.bfloat16)
     my_features = lax.dynamic_slice_in_dim(features, rep_pos * quarter, quarter, 0)
     mine = jnp.dot(my_pick, my_features, preferred_element_type=jnp.float32).astype(jnp.bfloat16)
-    halo = jnp.stack([from_behind(mine, "node", d) for d in (-1, 1, 2)])
-    gathered = lax.all_gather(halo, "rep", axis=0)
+    gathered = halo_call(mine, reps)
     gathered = gathered.reshape(reps, 3, per, size, feat)
 
     pick = (within[:, :, None] == spots[None, None, :]).astype(jnp.bfloat16)
@@ -346,25 +442,13 @@
     )
     full_back = full_back.reshape(blocks, size, feat)
     grad_scale = 1.0 / math.sqrt(rows_dev * lax.axis_size("node"))
-    weight_grad = sum_call(weight_part, grad_scale)
-
-    away = tile_call(
-        functools.partial(backward_kernel, (0, 2, 3), capacity),
-        (0, 2, 3), (reps, 3, per, size, feat), jnp.bfloat16, acc_shape, scalars + (full_back,), tile_set,
-    )
-    home = tile_call(
-        functools.partial(backward_kernel, (1,), capacity),
-        (1,), (reps, 1, per, size, feat), jnp.bfloat16, acc_shape, scalars + (full_back,), tile_set,
-    )
-    away = lax.psum_scatter(away.reshape(reps, 3 * quarter, feat), "rep", scatter_dimension=0)
-    home = lax.psum_scatter(home.reshape(rows_dev, feat), "rep", scatter_dimension=0, tiled=True)
-    away = away.reshape(3, quarter, feat)
-    total = home.astype(jnp.float32)
-    for j, d in enumerate((1, -1, -2)):
-        total = total + from_behind(away[j], "node", d).astype(jnp.float32)
-    feature_grad = lax.dot_general(
-        my_pick, total.astype(jnp.bfloat16), (((0,), (0,)), ((), ())), preferred_element_type=jnp.float32
-    ).astype(jnp.bfloat16)
+    terms = tile_call(
+        functools.partial(backward_kernel, (0, 2, 3, 1), capacity),
+        (0, 2, 3, 1), (reps, 4, per, size, feat), jnp.bfloat16, acc_shape, scalars + (full_back,), tile_set,
+    )
+    feature_grad, weight_grad = finish_call(
+        terms.reshape(reps, 4, quarter, feat), my_pick, weight_part, grad_scale
+    )
     return (activated, feature_grad, weight_grad)
 
 

time: 183 us -> 151 us (0.83)
  waiting for transfers between devices: 63.7 us -> 0 us
  Pallas kernels: 81.4 us -> 138 us
  between operations: 13.9 us -> 0.75 us
  starting transfers between devices: 11.9 us -> 0 us
    pallas_call x1 -> x2, Pallas kernels: 22.9 us -> 90.8 us  [the longest x1 49.8 us: finish_call(): pl.pallas_call(functools.partial(finish_kernel, nodes, reps, scale), out_...]
    reduce_scatter x2 -> x0, waiting for transfers between devices: 35.4 us -> none  [the longest x1 35.4 us: local(): lax.psum_scatter(away.reshape(reps, 3 * quarter, feat), 'rep', scatter_di...]
    all_gather x1 -> x0, waiting for transfers between devices: 18 us -> none  [local(): gathered = lax.all_gather(halo, 'rep', axis=0)]
    pallas_call x4 -> x3, Pallas kernels: 37.1 us -> 21.1 us  [tile_call(): pl.pallas_call(kernel, out_shape=jax.ShapeDtypeStruct(out_shape, out_dtyp...]
    ppermute x6 -> x0, starting transfers between devices: 11.8 us -> none  [from_behind(): lax.ppermute(block, axis, [((i - distance) % n, i) for i in range(n)])]
    ppermute x6 -> x0, waiting for transfers between devices: 10.2 us -> none  [from_behind(): lax.ppermute(block, axis, [((i - distance) % n, i) for i in range(n)])]
    pallas_call x1, Pallas kernels: 21.4 us -> 26.4 us  [dense_call(): pl.pallas_call(dense_kernel, out_shape=(jax.ShapeDtypeStruct(half, jnp.bf...]
    dot_general x1 -> x0, matrix products: 2.25 us -> none  [local(): lax.dot_general(my_pick, total.astype(jnp.bfloat16), (((0,), (0,)), ((),...]
  transfers between devices with their start and end apart: 9 -> 0, of which waited for: 4 -> 0; matrix products, arithmetic and copies ran while one was open for 4% -> 0% of each run, Pallas kernels for 21% -> 0%
where the time goes in v2:
time: 151 us; the launch traced here: 150 us
  Pallas kernels  138 us (91%)
  local copies, waits for them, and re-layouts  6.58 us (4%)
  matrix products  2.92 us (2%)
  other arithmetic  1.74 us (1%)
    pallas_call x1, Pallas kernels, finish_call(): pl.pallas_call(functools.partial(finish_kernel, nodes, reps, scale), out_...  49.8 us
    pallas_call x1, Pallas kernels, halo_call(): pl.pallas_call(functools.partial(halo_kernel, lax.axis_size('node')), out...  41.1 us
    pallas_call x1, Pallas kernels, dense_call(): pl.pallas_call(dense_kernel, out_shape=(jax.ShapeDtypeStruct(half, jnp.bf...  26.4 us
    pallas_call x3, Pallas kernels, tile_call(): pl.pallas_call(kernel, out_shape=jax.ShapeDtypeStruct(out_shape, out_dtyp...  21.1 us

profile of v2, /device:TPU:1, one launch (start us, length us, event | category | flops | bytes accessed | tf_op | source)
XLA Modules:
  0.0 150.3 jit_solution(10950567124677012623)
XLA Ops:
  0.6 0.0 copy-start
  0.6 0.0 copy-start.3
  0.7 0.0 copy-start.4
  0.7 0.8 add_select_fusion
  1.5 0.4 copy-done
  1.9 1.1 convolution_convert_fusion.mine
  2.9 41.1 %shard_map.103 = bf16[4,3,512,256]{3,2,1,0:T(8,128)(2,1)} custom-call(bf16[512,256]{1,0:T(8,128)(2,1)} %convolution_convert_fusion.mine), custom_call_target="tpu_custom_call" | custom-call | tf_op jit(solution)/shard_map/pallas_call | solution.py:232
  44.0 0.0 copy-done.3
  44.0 0.7 reshape.46.refs_1_.row_ref
  44.7 0.0 copy-done.4
  44.7 0.7 reshape.47.refs_2_.col_ref
  45.4 1.9 %fusion.2 = bf16[4,512,256]{2,1,0:T(8,128)(2,1)} fusion(bf16[4,512,256]{2,1,0:T(8,128)(2,1)S(1)} %bitcast.12, s32[4,512]{1,0:T(4,128)S(1)} %reshape.48), kind=kOutput, calls=%fused_computation.3 | convolution fusion | flops 538443776 | bytes 2105344 | tf_op jit(solution)/shard_map/qpi,qif->qpf/dot_general | solution.py:422
  47.2 5.0 %shard_map.104.refs_5_ = f32[16,128,256]{2,1,0:T(8,128)} custom-call(s32[4]{0:T(128)} %bitcast.23, s32[384]{0:T(512)} %reshape.46.refs_1_.row_ref, s32[384]{0:T(512)} %reshape.47.refs_2_.col_ref, bf16[4,96,128,128]{3,2,1,0:T(8,128)(2,1)} %bitcast.13, bf16[4,1,4,128,256]{4,3,2,1,0:T(8,128)(2,1)} %bitcast.20), custom_call_target="tpu_custom_call" | custom-call | tf_op jit(solution)/shard_map/pallas_call | solution.py:128
  52.2 7.1 %shard_map.105 = bf16[16,128,256]{2,1,0:T(8,128)(2,1)} custom-call(s32[4]{0:T(128)} %bitcast.24, s32[384]{0:T(512)} %reshape.46.refs_1_.row_ref, s32[384]{0:T(512)} %reshape.47.refs_2_.col_ref, bf16[4,96,128,128]{3,2,1,0:T(8,128)(2,1)} %bitcast.14, bf16[4,3,4,128,256]{4,3,2,1,0:T(8,128)(2,1)} %bitcast.17, f32[16,128,256]{2,1,0:T(8,128)} %shard_map.104.refs_5_), custom_call_target="tpu_custom_call" | custom-call | tf_op jit(solution)/shard_map/pallas_call | solution.py:128
  59.3 26.4 %shard_map.106 = (bf16[512,256]{1,0:T(8,128)(2,1)}, f32[256,256]{1,0:T(8,128)}, bf16[4,512,256]{2,1,0:T(8,128)(2,1)}) custom-call(bf16[4,512,256]{2,1,0:T(8,128)(2,1)} %bitcast.18, bf16[512,256]{1,0:T(8,128)(2,1)} %cot.1, bf16[256,256]{1,0:T(8,128)(2,1)} %weight.1), custom_call_target="tpu_custom_call" | custom-call | tf_op jit(solution)/shard_map/pallas_call | solution.py:377
  85.7 0.0 copy-start.2
  85.7 9.1 %shard_map.107 = bf16[4,4,4,128,256]{4,3,2,1,0:T(8,128)(2,1)} custom-call(s32[4]{0:T(128)} %bitcast.25, s32[384]{0:T(512)} %reshape.46.refs_1_.row_ref, s32[384]{0:T(512)} %reshape.47.refs_2_.col_ref, bf16[4,96,128,128]{3,2,1,0:T(8,128)(2,1)} %bitcast.15, bf16[16,128,256]{2,1,0:T(8,128)(2,1)} %bitcast.19), custom_call_target="tpu_custom_call" | custom-call | tf_op jit(solution)/shard_map/pallas_call | solution.py:128
  94.8 0.0 copy-start.1
  94.8 0.0 copy-done.2
  94.8 0.7 reshape.55.part
  95.5 1.0 fusion.3.pick
  96.5 49.8 %shard_map.108 = (bf16[512,256]{1,0:T(8,128)(2,1)}, f32[4,8,16,128]{3,2,1,0:T(8,128)}) custom-call(bf16[4,4,512,256]{3,2,1,0:T(8,128)(2,1)} %bitcast.16, bf16[512,512]{1,0:T(8,128)(2,1)} %fusion.3.pick, f32[4,8,16,128]{3,2,1,0:T(8,128)} %reshape.55.part), custom_call_target="tpu_custom_call" | custom-call | tf_op jit(solution)/shard_map/pallas_call | solution.py:341
  146.2 1.7 %reshape.56 = f32[256,256]{1,0:T(8,128)} reshape(f32[4,8,16,128]{3,2,1,0:T(8,128)} %get-tuple-element.12) | data formatting | bytes 524288 | tf_op jit(solution)/shard_map/reshape | solution.py:364
  148.0 0.0 copy-done.1
  148.0 0.7 copy.13
  148.7 1.7 %copy.14 = bf16[512,256]{1,0:T(8,128)(2,1)} copy(bf16[512,256]{1,0:T(8,128)(2,1)} %get-tuple-element.17) | data formatting | bytes 524288
  (2 shorter events, 0.0 us)
Async XLA Ops:
  0.6 1.2 copy-start
  0.6 43.4 %copy-start.3 = (s32[1,1,4,96]{3,2,1,0:T(4,128)S(1)}, s32[1,1,4,96]{3,2,1,0:T(4,128)}, u32[]{:S(2)}) copy-start(s32[1,1,4,96]{3,2,1,0:T(4,128)} %param.10) | copy-start | bytes 4612
  0.7 44.0 %copy-start.4 = (s32[1,1,4,96]{3,2,1,0:T(4,128)S(1)}, s32[1,1,4,96]{3,2,1,0:T(4,128)}, u32[]{:S(2)}) copy-start(s32[1,1,4,96]{3,2,1,0:T(4,128)} %param.11) | copy-start | bytes 4612
  85.7 9.1 %copy-start.2 = (f32[256,256]{1,0:T(8,128)S(1)}, f32[256,256]{1,0:T(8,128)}, u32[]{:S(2)}) copy-start(f32[256,256]{1,0:T(8,128)} %get-tuple-element.10) | copy-start | bytes 786436
  94.8 53.2 %copy-start.1 = (bf16[512,256]{1,0:T(8,128)(2,1)S(1)}, bf16[512,256]{1,0:T(8,128)(2,1)}, u32[]{:S(2)}) copy-start(bf16[512,256]{1,0:T(8,128)(2,1)} %get-tuple-element.16) | copy-start | bytes 786436
